TPU v7x, 32 devices: a whole 2x2x4 slice. The times are simulated.
32 devices in a mesh: dp: 16 (over z, y, x), head: 2 (over core).
Axes of the slice: x: 2, y: 2, z: 4, core: 2. Of those that a mesh axis runs over, the one named last changes fastest.
Arguments:
- patches: bfloat16 [16384, 768], P('dp'), may hold values from -6 to 6
- image_grids: int32 [96, 2], P('dp'), may hold values from 0 to 24, as said below
- out_grad: bfloat16 [16384, 768], P('dp'), may hold values from -6 to 6
- first_gain: float32 [768], replicated, may hold values from 0.5 to 1.5
- first_shift: float32 [768], replicated, may hold values from -1 to 1
- qkv_weight: bfloat16 [3, 768, 768], P(None, None, 'head'), may hold values from -0.21875 to 0.21875
- qkv_bias: float32 [3, 768], P(None, 'head'), may hold values from -1 to 1
- rope_freqs: float32 [2, 12, 32], P(None, 'head'), may hold values from -0.8 to 0.8
- proj_weight: bfloat16 [768, 768], P('head'), may hold values from -2.5 to 2.5
- proj_bias: float32 [768], replicated, may hold values from -1 to 1
- second_gain: float32 [768], replicated, may hold values from 0.5 to 1.5
- second_shift: float32 [768], replicated, may hold values from -1 to 1
- expand_weight: bfloat16 [768, 3072], P(None, 'head'), may hold values from -0.21875 to 0.21875
- expand_bias: float32 [3072], P('head'), may hold values from -1 to 1
- contract_weight: bfloat16 [3072, 768], P('head'), may hold values from -0.109375 to 0.109375
- contract_bias: float32 [768], replicated, may hold values from -1 to 1
Outputs:
- mixed_out: bfloat16 [16384, 768], P('dp')
- patches_grad: float32 [16384, 768], P('dp')
- qkv_weight_grad: float32 [3, 768, 768], P(None, 'dp', 'head')
- proj_weight_grad: float32 [768, 768], P('head', 'dp')
- expand_weight_grad: float32 [768, 3072], P('dp', 'head')
- contract_weight_grad: float32 [3072, 768], P('head', 'dp')
- first_gain_grad: float32 [768], replicated
- first_shift_grad: float32 [768], replicated
- qkv_bias_grad: float32 [3, 768], P(None, 'head')
- rope_freqs_grad: float32 [2, 12, 32], P(None, 'head')
- proj_bias_grad: float32 [768], replicated
- second_gain_grad: float32 [768], replicated
- second_shift_grad: float32 [768], replicated
- expand_bias_grad: float32 [3072], P('head')
- contract_bias_grad: float32 [768], replicated
Inputs may be any that keep to these rules, and one draw needn't show every extreme that they name: `image_grids`: every image is square with side 14, 20 or 24, height equal to width. In each block of 6 rows (one index of dp) the images come first and the empty slots (0, 0) after them; the images' patches total at most 1024, and every block has an empty slot.
All inputs are finite; a program needn't handle non-finite values.
Results may differ from a plain program's by a relative error of at most 0.012.
Values sent between devices are 32-bit elements; how exact they have to be, the bound alone decides.
A program may use at most 192 MiB of HBM per device.

v0:
```python
from functools import partial
import jax
import jax.numpy as jnp
from jax import lax
from jax.sharding import PartitionSpec as P

eps = 1e-06
masked_score = -1e30


def positions(image_grids, row_count):
    slot_count = image_grids.shape[0]
    image_len = image_grids[:, 0] * image_grids[:, 1]
    image_end = jnp.cumsum(image_len)
    image_start = image_end - image_len
    token_pos = jnp.arange(row_count, dtype=jnp.int32)
    segment = jnp.sum((token_pos[:, None] >= image_end[None, :]).astype(jnp.int32), axis=1)
    member = segment[:, None] == jnp.arange(slot_count, dtype=jnp.int32)[None, :]
    start_tok = jnp.sum(jnp.where(member, image_start[None, :], 0), axis=1)
    width_tok = jnp.sum(jnp.where(member, image_grids[None, :, 1], 0), axis=1)
    offset = token_pos - start_tok
    safe_width = jnp.maximum(width_tok, 1)
    real_row = segment < slot_count
    grid_row = jnp.where(real_row, offset // safe_width, 0).astype(jnp.float32)
    grid_col = jnp.where(real_row, offset % safe_width, 0).astype(jnp.float32)
    return (segment, grid_row, grid_col, real_row.astype(jnp.float32))


def layer_norm_parts(source, gain, shift):
    mean_val = jnp.mean(source, axis=-1, keepdims=True)
    centred = source - mean_val
    inv_dev = lax.rsqrt(jnp.mean(centred * centred, axis=-1, keepdims=True) + eps)
    unit = centred * inv_dev
    return (unit * gain + shift, unit, inv_dev)


def norm_back(upstream, unit, inv_dev, gain):
    scaled = upstream * gain
    return inv_dev * (
        scaled
        - jnp.mean(scaled, axis=-1, keepdims=True)
        - unit * jnp.mean(scaled * unit, axis=-1, keepdims=True)
    )


def rotate_pairs(source, cosine, sine_val):
    row_count = source.shape[0]
    head_count = cosine.shape[1]
    half_size = cosine.shape[2]
    shaped = source.reshape(row_count, head_count, 2, half_size)
    first_half = shaped[:, :, 0]
    second_half = shaped[:, :, 1]
    turned = jnp.stack(
        [
            first_half * cosine - second_half * sine_val,
            first_half * sine_val + second_half * cosine,
        ],
        axis=2,
    )
    return turned.reshape(row_count, head_count * 2 * half_size)


def rotate_back(grad_rot, turned, cosine, sine_val):
    row_count = grad_rot.shape[0]
    head_count = cosine.shape[1]
    half_size = cosine.shape[2]
    grad_shaped = grad_rot.reshape(row_count, head_count, 2, half_size)
    turn_shaped = turned.reshape(row_count, head_count, 2, half_size)
    grad_first = grad_shaped[:, :, 0]
    grad_second = grad_shaped[:, :, 1]
    input_grad = jnp.stack(
        [
            grad_first * cosine + grad_second * sine_val,
            grad_second * cosine - grad_first * sine_val,
        ],
        axis=2,
    )
    angle_grad = grad_second * turn_shaped[:, :, 0] - grad_first * turn_shaped[:, :, 1]
    return (input_grad.reshape(row_count, head_count * 2 * half_size), angle_grad)


def attend_forward(query_low, key_low, value_low, segment, head_count):
    row_count = query_low.shape[0]
    head_size = query_low.shape[1] // head_count
    block = min(512, row_count)
    count = row_count // block
    score_scale = head_size ** (-0.5)
    key_heads = key_low.reshape(row_count, head_count, head_size)
    value_heads = value_low.reshape(row_count, head_count, head_size)
    query_blocks = query_low.reshape(count, block, head_count, head_size)
    segment_blocks = segment.reshape(count, block)

    def one_block(block_item):
        query_block, segment_query = block_item
        scores = (
            jnp.einsum("qhd,khd->hqk", query_block, key_heads, preferred_element_type=jnp.float32)
            * score_scale
        )
        same_image = (segment_query[:, None] == segment[None, :])[None]
        scores = jnp.where(same_image, scores, masked_score)
        row_max = jnp.max(scores, axis=-1, keepdims=True)
        exp_scores = jnp.exp(scores - row_max)
        row_total = jnp.sum(exp_scores, axis=-1, keepdims=True)
        probabilities = (exp_scores / row_total).astype(jnp.bfloat16)
        block_out = jnp.einsum(
            "hqk,khd->qhd", probabilities, value_heads, preferred_element_type=jnp.float32
        )
        return (block_out, (row_max + jnp.log(row_total))[..., 0])

    block_outs, log_sum = lax.map(one_block, (query_blocks, segment_blocks))
    return (block_outs.reshape(row_count, head_count * head_size), log_sum)


def attend_backward(query_low, key_low, value_low, attended_grad, log_sum, segment, head_count):
    row_count = query_low.shape[0]
    head_size = query_low.shape[1] // head_count
    block = min(512, row_count)
    count = row_count // block
    score_scale = head_size ** (-0.5)
    key_heads = key_low.reshape(row_count, head_count, head_size)
    value_heads = value_low.reshape(row_count, head_count, head_size)
    query_blocks = query_low.reshape(count, block, head_count, head_size)
    grad_blocks = attended_grad.reshape(count, block, head_count, head_size)
    segment_blocks = segment.reshape(count, block)

    def one_block(carry, block_item):
        key_grad, value_grad = carry
        query_block, grad_block, log_block, segment_query = block_item
        scores = (
            jnp.einsum("qhd,khd->hqk", query_block, key_heads, preferred_element_type=jnp.float32)
            * score_scale
        )
        same_image = (segment_query[:, None] == segment[None, :])[None]
        scores = jnp.where(same_image, scores, masked_score)
        probabilities = jnp.exp(scores - log_block[..., None])
        value_grad = value_grad + jnp.einsum(
            "hqk,qhd->khd",
            probabilities.astype(jnp.bfloat16),
            grad_block,
            preferred_element_type=jnp.float32,
        )
        prob_grad = jnp.einsum(
            "qhd,khd->hqk", grad_block, value_heads, preferred_element_type=jnp.float32
        )
        inner = jnp.sum(probabilities * prob_grad, axis=-1, keepdims=True)
        score_grad = (probabilities * (prob_grad - inner)).astype(jnp.bfloat16)
        query_grad = (
            jnp.einsum("hqk,khd->qhd", score_grad, key_heads, preferred_element_type=jnp.float32)
            * score_scale
        )
        key_grad = (
            key_grad
            + jnp.einsum(
                "hqk,qhd->khd", score_grad, query_block, preferred_element_type=jnp.float32
            )
            * score_scale
        )
        return ((key_grad, value_grad), query_grad)

    empty = jnp.zeros((row_count, head_count, head_size), jnp.float32)
    (key_grad, value_grad), query_grads = lax.scan(
        one_block, (empty, empty), (query_blocks, grad_blocks, log_sum, segment_blocks)
    )
    width = head_count * head_size
    return (
        query_grads.reshape(row_count, width),
        key_grad.reshape(row_count, width),
        value_grad.reshape(row_count, width),
    )


def run_forward(source, params, cosine, sine_val, segment):
    (
        gain_one,
        shift_one,
        weight_qkv,
        bias_qkv,
        weight_proj,
        bias_proj,
        gain_two,
        shift_two,
        weight_expand,
        bias_expand,
        weight_contract,
        bias_contract,
    ) = params
    start_value = source.astype(jnp.float32)
    norm_one, unit_one, inv_one = layer_norm_parts(start_value, gain_one, shift_one)
    normed_first = norm_one.astype(jnp.bfloat16)
    projected = (
        jnp.einsum("td,kdh->kth", normed_first, weight_qkv, preferred_element_type=jnp.float32)
        + bias_qkv[:, None, :]
    )
    query_rot = rotate_pairs(projected[0], cosine, sine_val)
    key_rot = rotate_pairs(projected[1], cosine, sine_val)
    query_low = query_rot.astype(jnp.bfloat16)
    key_low = key_rot.astype(jnp.bfloat16)
    value_low = projected[2].astype(jnp.bfloat16)
    attended, log_sum = attend_forward(query_low, key_low, value_low, segment, cosine.shape[1])
    attended_low = attended.astype(jnp.bfloat16)
    branch = (
        lax.psum(jnp.dot(attended_low, weight_proj, preferred_element_type=jnp.float32), "head")
        + bias_proj
    )
    middle = start_value + branch
    norm_two, unit_two, inv_two = layer_norm_parts(middle, gain_two, shift_two)
    normed_second = norm_two.astype(jnp.bfloat16)
    hidden = jnp.dot(normed_second, weight_expand, preferred_element_type=jnp.float32) + bias_expand
    active_low = jax.nn.gelu(hidden, approximate=False).astype(jnp.bfloat16)
    branch_two = (
        lax.psum(jnp.dot(active_low, weight_contract, preferred_element_type=jnp.float32), "head")
        + bias_contract
    )
    outcome = middle + branch_two
    return (
        unit_one,
        inv_one,
        normed_first,
        query_rot,
        key_rot,
        query_low,
        key_low,
        value_low,
        log_sum,
        attended_low,
        unit_two,
        inv_two,
        normed_second,
        hidden,
        active_low,
        outcome,
    )


def body(
    patches,
    image_grids,
    out_grad,
    first_gain,
    first_shift,
    qkv_weight,
    qkv_bias,
    rope_freqs,
    proj_weight,
    proj_bias,
    second_gain,
    second_shift,
    expand_weight,
    expand_bias,
    contract_weight,
    contract_bias,
):
    row_count = patches.shape[0]
    head_count = rope_freqs.shape[1]
    segment, grid_row, grid_col, real_row = positions(image_grids, row_count)
    turn_angle = (
        grid_row[:, None, None] * rope_freqs[0][None]
        + grid_col[:, None, None] * rope_freqs[1][None]
    )
    cosine = jnp.cos(turn_angle)
    sine_val = jnp.sin(turn_angle)
    params = (
        first_gain,
        first_shift,
        qkv_weight,
        qkv_bias,
        proj_weight,
        proj_bias,
        second_gain,
        second_shift,
        expand_weight,
        expand_bias,
        contract_weight,
        contract_bias,
    )
    saved = run_forward(patches, params, cosine, sine_val, segment)
    mixed_out = saved[15].astype(jnp.bfloat16)
    fresh = lax.optimization_barrier((patches, params, mixed_out))
    saved = run_forward(fresh[0], fresh[1], cosine, sine_val, segment)
    (
        unit_one,
        inv_one,
        normed_first,
        query_rot,
        key_rot,
        query_low,
        key_low,
        value_low,
        log_sum,
        attended_low,
        unit_two,
        inv_two,
        normed_second,
        hidden,
        active_low,
        outcome,
    ) = saved
    cot_low = out_grad * real_row[:, None].astype(jnp.bfloat16)
    cot_value = cot_low.astype(jnp.float32)
    contract_bias_grad = jnp.sum(cot_value, axis=0)
    contract_grad = jnp.einsum("tf,td->fd", active_low, cot_low, preferred_element_type=jnp.float32)
    active_grad = jnp.einsum(
        "td,fd->tf", cot_low, contract_weight, preferred_element_type=jnp.float32
    )
    gelu_value, gelu_pull = jax.vjp(partial(jax.nn.gelu, approximate=False), hidden)
    hidden_grad = gelu_pull(active_grad)[0].astype(jnp.bfloat16)
    expand_bias_grad = jnp.sum(hidden_grad.astype(jnp.float32), axis=0)
    expand_grad = jnp.einsum(
        "td,tf->df", normed_second, hidden_grad, preferred_element_type=jnp.float32
    )
    second_grad = lax.psum(
        jnp.einsum("tf,df->td", hidden_grad, expand_weight, preferred_element_type=jnp.float32),
        "head",
    )
    second_gain_grad = jnp.sum(second_grad * unit_two, axis=0)
    second_shift_grad = jnp.sum(second_grad, axis=0)
    middle_grad = cot_value + norm_back(second_grad, unit_two, inv_two, second_gain)
    middle_low = middle_grad.astype(jnp.bfloat16)
    proj_bias_grad = jnp.sum(middle_low.astype(jnp.float32), axis=0)
    proj_grad = jnp.einsum(
        "th,td->hd", attended_low, middle_low, preferred_element_type=jnp.float32
    )
    attended_grad = jnp.einsum(
        "td,hd->th", middle_low, proj_weight, preferred_element_type=jnp.float32
    ).astype(jnp.bfloat16)
    query_rot_grad, key_rot_grad, value_grad = attend_backward(
        query_low, key_low, value_low, attended_grad, log_sum, segment, head_count
    )
    query_in_grad, query_angle = rotate_back(query_rot_grad, query_rot, cosine, sine_val)
    key_in_grad, key_angle = rotate_back(key_rot_grad, key_rot, cosine, sine_val)
    angle_grad = query_angle + key_angle
    rope_freqs_grad = jnp.stack(
        [
            jnp.einsum("t,thf->hf", grid_row, angle_grad, precision=lax.Precision.HIGHEST),
            jnp.einsum("t,thf->hf", grid_col, angle_grad, precision=lax.Precision.HIGHEST),
        ]
    )
    qkv_grad_low = jnp.stack([query_in_grad, key_in_grad, value_grad]).astype(jnp.bfloat16)
    qkv_bias_grad = jnp.sum(qkv_grad_low.astype(jnp.float32), axis=1)
    qkv_grad = jnp.einsum(
        "td,kth->kdh", normed_first, qkv_grad_low, preferred_element_type=jnp.float32
    )
    first_grad = lax.psum(
        jnp.einsum("kth,kdh->td", qkv_grad_low, qkv_weight, preferred_element_type=jnp.float32),
        "head",
    )
    first_gain_grad = jnp.sum(first_grad * unit_one, axis=0)
    first_shift_grad = jnp.sum(first_grad, axis=0)
    patches_grad = middle_grad + norm_back(first_grad, unit_one, inv_one, first_gain)
    qkv_sum, proj_sum, expand_sum, contract_sum = (
        lax.psum_scatter(qkv_grad, "dp", scatter_dimension=1, tiled=True),
        lax.psum_scatter(proj_grad, "dp", scatter_dimension=1, tiled=True),
        lax.psum_scatter(expand_grad, "dp", scatter_dimension=0, tiled=True),
        lax.psum_scatter(contract_grad, "dp", scatter_dimension=1, tiled=True),
    )
    (
        first_gain_sum,
        first_shift_sum,
        qkv_bias_sum,
        rope_freqs_sum,
        proj_bias_sum,
        second_gain_sum,
        second_shift_sum,
        expand_bias_sum,
        contract_bias_sum,
    ) = lax.psum(
        (
            first_gain_grad,
            first_shift_grad,
            qkv_bias_grad,
            rope_freqs_grad,
            proj_bias_grad,
            second_gain_grad,
            second_shift_grad,
            expand_bias_grad,
            contract_bias_grad,
        ),
        "dp",
    )
    return (
        mixed_out,
        patches_grad,
        qkv_sum,
        proj_sum,
        expand_sum,
        contract_sum,
        first_gain_sum,
        first_shift_sum,
        qkv_bias_sum,
        rope_freqs_sum,
        proj_bias_sum,
        second_gain_sum,
        second_shift_sum,
        expand_bias_sum,
        contract_bias_sum,
    )


def solution(mesh):
    in_specs = (
        P("dp", None),
        P("dp", None),
        P("dp", None),
        P(),
        P(),
        P(None, None, "head"),
        P(None, "head"),
        P(None, "head", None),
        P("head", None),
        P(),
        P(),
        P(),
        P(None, "head"),
        P("head"),
        P("head", None),
        P(),
    )
    out_specs = (
        P("dp", None),
        P("dp", None),
        P(None, "dp", "head"),
        P("head", "dp"),
        P("dp", "head"),
        P("head", "dp"),
        P(),
        P(),
        P(None, "head"),
        P(None, "head", None),
        P(),
        P(),
        P(),
        P("head"),
        P(),
    )
    return jax.shard_map(body, mesh=mesh, in_specs=in_specs, out_specs=out_specs, check_vma=False)
```

profile of v0, /device:TPU:0, one launch (start us, length us, event | category | flops | bytes accessed | tf_op | source)
XLA Modules:
  0.0 1078.4 jit_solution(5829515903000823336)
XLA Ops:
  13.6 3.8 add_bitcast_fusion.1
  19.4 4.5 subtract_convert_fusion.1
  29.6 64.2 %while.37 = (s32[]{:T(128)}, bf16[2,512,6,64]{1,3,2,0:T(8,128)(2,1)}, s32[2,512]{1,0:T(2,128)S(1)}, s32[1024]{0:T(1024)S(1)}, bf16[2,512,6,64]{1,3,2,0:T(8,128)(...) while((s32[]{:T(128)}, bf16[2,512,6,64]{1,3,2,0:T(8,128)(2,1)}, ...), condition=%wide.region_9.10_spmd, body=%wide.region_6.9_spmd.sunk | while | flops 830997504 | bytes 63609020 | solution.py:110
  30.0 7.4 fusion.243
  37.4 16.7 %fusion.244 = (f32[6,512]{1,0:T(8,128)S(1)}, f32[6,512,1024]{2,1,0:T(8,128)}) fusion(f32[6,512,1024]{2,1,0:T(8,128)} %fusion.243, pred[512,1024]{1,0:T(8,128)(4,1)S(1)} %broadcast_compare_fusion.8), kind=kOutput, calls=%fused_computation.303.clone.1 | output fusion | flops 18875392 | bytes 25702400 | tf_op jit(solution)/shard_map/while/body/eval_jaxpr/sub | solution.py:102
  54.1 6.7 fusion.245
  62.1 7.4 fusion.243
  69.5 16.7 %fusion.244 = (f32[6,512]{1,0:T(8,128)S(1)}, f32[6,512,1024]{2,1,0:T(8,128)}) fusion(f32[6,512,1024]{2,1,0:T(8,128)} %fusion.243, pred[512,1024]{1,0:T(8,128)(4,1)S(1)} %broadcast_compare_fusion.8), kind=kOutput, calls=%fused_computation.303.clone.1 | output fusion | flops 18875392 | bytes 25702400 | tf_op jit(solution)/shard_map/while/body/eval_jaxpr/sub | solution.py:102
  86.2 6.7 fusion.245
  98.7 26.1 %all-reduce.9.cloned.1.call-done = f32[1024,768]{1,0:T(8,128)} async-done(((f32[1024,768]{1,0:T(8,128)}), f32[1024,768]{1,0:T(8,128)}) %all-reduce.9.cloned.1.call-update) | async-done | bytes 3145744 | tf_op jit(solution)/shard_map/psum | solution.py:202
  129.5 21.6 %fusion.87 = f32[1024,768]{1,0:T(8,128)} fusion(bf16[1536,768]{1,0:T(8,128)(2,1)} %param.36, bf16[768,1536]{1,0:T(8,128)(2,1)S(1)} %copy-done, f32[1536]{0:T(1024)S(1)} %copy-done.70, f32[768]{0:T(1024)S(1)} %copy-done.77, f32[768]{0:T(1024)S(1)} %copy-done.56, f32[1024]{0:T(1024)S(1)} %add_rsqrt_fusion.2, f32[1024]{0:T(1024)S(1)} %broadcast_multiply_fusion.6, ...), kind=kOutput, calls=%fused_computation.148 | convolution fusion | flops 4941938688 | bytes 12606464 | tf_op jit(solution)/shard_map/dot_general | solution.py:211
  151.2 24.6 %all-reduce.11.cloned.1.call-done = f32[1024,768]{1,0:T(8,128)} async-done(((f32[1024,768]{1,0:T(8,128)}), f32[1024,768]{1,0:T(8,128)}) %all-reduce.11.cloned.1.call-update) | async-done | bytes 3145744 | tf_op jit(solution)/shard_map/psum | solution.py:211
  175.8 5.1 add_convert_fusion.2
  187.0 4.0 fusion.123
  198.6 25.5 %while.38 = (s32[]{:T(128)}, bf16[2,512,6,64]{1,3,2,0:T(8,128)(2,1)}, f32[2,6,512]{2,1,0:T(8,128)S(1)}, s32[2,512]{1,0:T(2,128)S(1)}, s32[1024]{0:T(1024)S(1)}, ...) while((s32[]{:T(128)}, ...), condition=%wide.region_19.20_spmd, body=%wide.region_16.19_spmd.sunk | while | flops 843576320 | bytes 52164808 | solution.py:110
  202.4 3.6 fusion.249
  206.1 4.4 fusion.250
  218.8 4.4 fusion.250
  230.1 24.4 %all-reduce.13.cloned.1.call-done = f32[1024,768]{1,0:T(8,128)} async-done(((f32[1024,768]{1,0:T(8,128)}), f32[1024,768]{1,0:T(8,128)}) %all-reduce.13.cloned.1.call-update) | async-done | bytes 3145744 | tf_op jit(solution)/shard_map/psum | solution.py:202
  257.9 15.1 %fusion.51 = (f32[1024,1536]{1,0:T(8,128)S(1)}, f32[1024,1536]{1,0:T(8,128)S(1)}) fusion(f32[1536]{0:T(1024)S(1)} %copy-done.70, bf16[768,1536]{1,0:T(8,128)(2,1)S(1)} %copy-done, f32[1024,768]{1,0:T(8,128)S(1)} %get-tuple-element.484, f32[768]{0:T(1024)S(1)} %copy-done.77, f32[768]{0:T(1024)S(1)} %copy-done.56, f32[1024]{0:T(1024)S(1)} %add_rsqrt_fusion, ...), kind=kOutput, calls=%fused_computation.70 | convolution fusion | flops 2518941696 | bytes 18108416 | tf_op jit(solution)/shard_map/dot_general | solution.py:208
  273.1 5.6 convert_reduce_fusion
  280.5 4.3 fusion.186
  284.9 24.6 %all-reduce.15.cloned.1.call-done = f32[1024,768]{1,0:T(8,128)} async-done(((f32[1024,768]{1,0:T(8,128)}), f32[1024,768]{1,0:T(8,128)}) %all-reduce.15.cloned.1.call-update) | async-done | bytes 3145744 | tf_op jit(solution)/shard_map/psum | solution.py:311
  309.4 4.4 multiply_reduce_fusion.1
  314.1 3.9 convert_reduce_fusion.5
  329.2 87.9 %while.39 = (s32[]{:T(128)}, f32[1024,6,64]{0,2,1:T(8,128)}, f32[1024,6,64]{0,2,1:T(8,128)}, f32[2,512,6,64]{1,0,3,2:T(2,128)}, bf16[2,512,6,64]{1,3,2,0:T(8,128...) while((s32[]{:T(128)}, f32[1024,6,64]{0,2,1:T(8,128)}, ...), condition=%wide.region_28.29_spmd.clone, body=%wide.region_26.28_spmd.clone.sunk | while | flops 2063135744 | bytes 132749616 | solution.py:161
  333.0 4.6 bitcast_add_fusion.5
  337.6 7.1 multiply_reduce_fusion.8
  344.7 6.9 multiply_convert_fusion.4
  357.9 15.0 %dynamic_update_slice.25 = f32[2,512,6,64]{1,0,3,2:T(2,128)} dynamic-update-slice(f32[2,512,6,64]{1,0,3,2:T(2,128)} %get-tuple-element.762, f32[1,512,6,64]{1,0,3,2:T(1,128)} %copy.267, s32[]{:T(128)S(6)} %copy.295, s32[]{:T(128)} %constant.51.clone.1..sunk, s32[]{:T(128)} %constant.51.clone.1..sunk, s32[]{:T(128)} %constant.51.clone.1..sunk) | dynamic-update-slice | bytes 1572868 | tf_op jit(solution)/shard_map/while/body/jit(dynamic_update_index_in_dim)/dynamic_update_slice | solution.py:110
  376.1 5.8 bitcast_add_fusion.5
  381.9 7.1 multiply_reduce_fusion.8
  389.0 6.9 multiply_convert_fusion.4
  402.2 15.0 %dynamic_update_slice.25 = f32[2,512,6,64]{1,0,3,2:T(2,128)} dynamic-update-slice(f32[2,512,6,64]{1,0,3,2:T(2,128)} %get-tuple-element.762, f32[1,512,6,64]{1,0,3,2:T(1,128)} %copy.267, s32[]{:T(128)S(6)} %copy.295, s32[]{:T(128)} %constant.51.clone.1..sunk, s32[]{:T(128)} %constant.51.clone.1..sunk, s32[]{:T(128)} %constant.51.clone.1..sunk) | dynamic-update-slice | bytes 1572868 | tf_op jit(solution)/shard_map/while/body/jit(dynamic_update_index_in_dim)/dynamic_update_slice | solution.py:110
  420.7 5.4 fusion.119
  438.0 5.9 convolution_bitcast_fusion.1
  444.6 6.1 convolution_bitcast_fusion
  450.7 6.5 copy.223
  458.3 3.9 fusion.142
  462.6 11.4 %fusion.84 = f32[1536,768]{0,1:T(8,128)} fusion(f32[1024,1536]{1,0:T(8,128)} %copy-done.80, f32[1024,1536]{1,0:T(8,128)} %copy-done.81, f32[1536]{0:T(1024)S(1)} %copy-done.71, bf16[1024,768]{1,0:T(8,128)(2,1)} %param.24, bf16[1024]{0:T(1024)(128)(2,1)S(1)} %copy-done.64), kind=kOutput, calls=%fused_computation.133 | convolution fusion | flops 2422996992 | bytes 18882560 | tf_op jit(solution)/shard_map/tf,td->fd/dot_general | solution.py:301
  474.7 7.9 fusion.177
  484.6 5.8 fusion.111
  497.5 79.5 %all-reduce.1 = (f32[768]{0:T(1024)}, f32[768]{0:T(1024)}, f32[3,384]{1,0:T(4,128)}, f32[2,6,32]{2,1,0:T(8,128)S(1)}, f32[768]{0:T(1024)}, /*index=5*/f32[768]{0...) all-reduce(f32[768]{0:T(1024)S(1)} %get-tuple-element.410, ...), channel_id=1, replica_groups=mesh['dp'=16,'head'=2] {'dp'}, use_global_device_ids=true, to_apply=%region_37.38 | all-reduce | flops 7680 | bytes 61440 | tf_op jit(solution)/shard_map/psum | solution.py:366
  577.6 5.0 fusion.77
  582.6 72.6 %all-reduce.19.cloned.1.call-done = f32[3,768,384]{2,0,1:T(4,128)} async-done(((f32[3,768,384]{2,0,1:T(4,128)}), f32[3,768,384]{2,0,1:T(4,128)}) %all-reduce.19.cloned.1.call-update) | async-done | bytes 3538960
  656.9 127.7 %reduce-scatter.4.cloned.1.call-done = f32[384,48]{0,1:T(8,128)} async-done(((f32[384,768]{0,1:T(8,128)}), f32[384,48]{0,1:T(8,128)}) %reduce-scatter.4.cloned.1.call-update) | async-done | bytes 73744 | tf_op jit(solution)/shard_map/reduce_scatter | solution.py:352
  784.6 143.5 %reduce-scatter.8.cloned.1.call-done = f32[1536,48]{0,1:T(8,128)} async-done(((f32[1536,768]{0,1:T(8,128)}), f32[1536,48]{0,1:T(8,128)}) %reduce-scatter.8.cloned.1.call-update) | async-done | bytes 294928 | tf_op jit(solution)/shard_map/reduce_scatter | solution.py:354
  928.1 143.6 %reduce-scatter.6.cloned.1.call-done = f32[48,1536]{1,0:T(8,128)} async-done(((f32[768,1536]{1,0:T(8,128)}), f32[48,1536]{1,0:T(8,128)}) %reduce-scatter.6.cloned.1.call-update) | async-done | bytes 294928 | tf_op jit(solution)/shard_map/reduce_scatter | solution.py:353
  (315 shorter events, 122.5 us)
Async XLA Ops:
  7.2 122.3 %copy-start = (bf16[768,1536]{1,0:T(8,128)(2,1)S(1)}, bf16[768,1536]{1,0:T(8,128)(2,1)}, u32[]{:S(2)}) copy-start(bf16[768,1536]{1,0:T(8,128)(2,1)} %param.34) | copy-start | bytes 7077892
  7.2 6.4 copy-start.58
  7.2 6.4 copy-start.72
  7.2 6.4 copy-start.74
  7.2 117.6 %all-reduce.9.cloned.1.call-start = ((), (), s32[]{:S(2)}) async-start(), calls=%async_computation.3 | async-start | bytes 6291456 | tf_op jit(solution)/shard_map/psum | solution.py:202
  9.7 3.9 copy-start.1
  19.1 4.8 copy-start.39
  19.2 4.8 copy-start.42
  19.4 4.5 copy-start.33
  19.4 4.5 copy-start.36
  37.4 16.7 %copy-start.25 = (bf16[2,512,6,64]{1,3,2,0:T(8,128)(2,1)S(1)}, bf16[2,512,6,64]{1,3,2,0:T(8,128)(2,1)}, u32[]{:S(2)}) copy-start(bf16[2,512,6,64]{1,3,2,0:T(8,128)(2,1)} %get-tuple-element.704) | copy-start | bytes 2359300 | tf_op jit(solution)/shard_map/while
  37.4 16.7 %copy-start.32 = (bf16[1024,6,64]{0,2,1:T(8,128)(2,1)S(1)}, bf16[1024,6,64]{0,2,1:T(8,128)(2,1)}, u32[]{:S(2)}) copy-start(bf16[1024,6,64]{0,2,1:T(8,128)(2,1)} %get-tuple-element.717) | copy-start | bytes 2359300 | tf_op jit(solution)/shard_map/while
  69.5 16.7 %copy-start.25 = (bf16[2,512,6,64]{1,3,2,0:T(8,128)(2,1)S(1)}, bf16[2,512,6,64]{1,3,2,0:T(8,128)(2,1)}, u32[]{:S(2)}) copy-start(bf16[2,512,6,64]{1,3,2,0:T(8,128)(2,1)} %get-tuple-element.704) | copy-start | bytes 2359300 | tf_op jit(solution)/shard_map/while
  69.5 16.7 %copy-start.32 = (bf16[1024,6,64]{0,2,1:T(8,128)(2,1)S(1)}, bf16[1024,6,64]{0,2,1:T(8,128)(2,1)}, u32[]{:S(2)}) copy-start(bf16[1024,6,64]{0,2,1:T(8,128)(2,1)} %get-tuple-element.717) | copy-start | bytes 2359300 | tf_op jit(solution)/shard_map/while
  96.0 28.9 %copy-start.49 = (f32[768]{0:T(1024)S(1)}, f32[768]{0:T(1024)}, u32[]{:S(2)}) copy-start(f32[768]{0:T(1024)} %param.31) | copy-start | bytes 9220
  98.7 77.1 %all-reduce.11.cloned.1.call-start = ((), (), s32[]{:S(2)}) async-start(), calls=%async_computation.4 | async-start | bytes 6291456 | tf_op jit(solution)/shard_map/psum | solution.py:211
  151.1 24.7 %copy-start.67 = (f32[768]{0:T(1024)S(1)}, f32[768]{0:T(1024)}, u32[]{:S(2)}) copy-start(f32[768]{0:T(1024)} %param.37) | copy-start | bytes 9220
  151.1 103.4 %all-reduce.13.cloned.1.call-start = ((), (), s32[]{:S(2)}) async-start(), calls=%async_computation.5 | async-start | bytes 6291456 | tf_op jit(solution)/shard_map/psum | solution.py:202
  175.8 5.1 copy-start.3
  181.2 4.0 copy-start.45
  186.7 4.4 copy-start.14
  186.7 4.4 copy-start.15
  229.9 79.5 %all-reduce.15.cloned.1.call-start = ((), (), s32[]{:S(2)}) async-start(), calls=%async_computation.6 | async-start | bytes 6291456 | tf_op jit(solution)/shard_map/psum | solution.py:311
  257.4 15.7 %copy-start.9 = (f32[1024,768]{1,0:T(8,128)}, f32[1024,768]{1,0:T(8,128)S(1)}, u32[]{:S(2)}) copy-start(f32[1024,768]{1,0:T(8,128)S(1)} %get-tuple-element.484) | copy-start | bytes 9437188
  257.4 56.5 %copy-start.47 = (f32[1024]{0:T(1024)}, f32[1024]{0:T(1024)S(1)}, u32[]{:S(2)}) copy-start(f32[1024]{0:T(1024)S(1)} %broadcast_multiply_fusion.4) | copy-start | bytes 12292
  257.9 56.0 %copy-start.52 = (f32[1024]{0:T(1024)}, f32[1024]{0:T(1024)S(1)}, u32[]{:S(2)}) copy-start(f32[1024]{0:T(1024)S(1)} %add_rsqrt_fusion) | copy-start | bytes 12292
  257.9 15.2 %copy-start.31 = (bf16[1024,768]{1,0:T(8,128)(2,1)S(1)}, bf16[1024,768]{1,0:T(8,128)(2,1)}, u32[]{:S(2)}) copy-start(bf16[1024,768]{1,0:T(8,128)(2,1)} %param.24) | copy-start | bytes 4718596
  257.9 15.2 %copy-start.63 = (bf16[1024]{0:T(1024)(128)(2,1)S(1)}, bf16[1024]{0:T(1024)(128)(2,1)}, u32[]{:S(2)}) copy-start(bf16[1024]{0:T(1024)(128)(2,1)} %get-tuple-element.481) | copy-start | bytes 6148
  257.9 15.2 %copy-start.68 = (bf16[1536,768]{1,0:T(8,128)(2,1)S(1)}, bf16[1536,768]{1,0:T(8,128)(2,1)}, u32[]{:S(2)}) copy-start(bf16[1536,768]{1,0:T(8,128)(2,1)} %param.36) | copy-start | bytes 7077892
  273.1 5.7 copy-start.80
  273.1 5.7 copy-start.81
  284.8 209.4 %all-reduce.17.cloned.1.call-start = ((), (), s32[]{:S(2)}) async-start(), calls=%async_computation.7 | async-start | bytes 6291456 | tf_op jit(solution)/shard_map/psum | solution.py:343
  309.4 4.5 copy-start.10
  309.4 4.7 copy-start.16
  314.1 5.5 copy-start.22
  333.0 4.6 copy-start.12
  376.1 5.8 copy-start.12
  420.7 5.4 copy-start.6
  433.1 4.9 copy-start.27
  443.9 211.3 %all-reduce.19.cloned.1.call-start = ((), (), s32[]{:S(2)}) async-start(), calls=%async_computation.11 | async-start | bytes 9437184
  457.2 5.3 copy-start.64
  457.2 5.3 copy-start.71
  457.2 327.3 %reduce-scatter.4.cloned.1.call-start = ((), (), s32[]{:S(2)}) async-start(), calls=%async_computation.8 | async-start | bytes 1253376 | tf_op jit(solution)/shard_map/reduce_scatter | solution.py:352
  462.3 465.8 %reduce-scatter.8.cloned.1.call-start = ((), (), s32[]{:S(2)}) async-start(), calls=%async_computation.10 | async-start | bytes 5013504 | tf_op jit(solution)/shard_map/reduce_scatter | solution.py:354
  474.0 597.6 %reduce-scatter.6.cloned.1.call-start = ((), (), s32[]{:S(2)}) async-start(), calls=%async_computation.9 | async-start | bytes 5013504 | tf_op jit(solution)/shard_map/reduce_scatter | solution.py:353
  484.5 9.2 copy-start.28
  484.5 9.2 copy-start.29
  484.6 9.2 copy-start.30
  (55 other events, 107.4 us)
Sparse Core Ops, SparseCore 0:
  98.8 26.0 all-reduce.8
  151.2 24.5 all-reduce.10
  230.0 24.4 all-reduce.12
  284.9 24.4 all-reduce.14
  444.0 24.4 all-reduce.16
  474.1 181.0 all-reduce.18
  660.5 124.0 reduce-scatter.3
  790.3 137.6 reduce-scatter.7
  933.8 137.7 reduce-scatter.5
where the time goes:
time: 1090 us; the launch traced here: 1080 us
  waiting for transfers between devices  587 us (54%)
  matrix products  180 us (17%)
  other arithmetic  121 us (11%)
  local copies, waits for them, and re-layouts  93.3 us (9%)
  blocking collectives  79.5 us (7%)
  between operations  15.7 us (1%)
    reduce_scatter x1, waiting for transfers between devices, body(): lax.psum_scatter(expand_grad, 'dp', scatter_dimension=0, tiled=True)  144 us
    reduce_scatter x1, waiting for transfers between devices, body(): lax.psum_scatter(contract_grad, 'dp', scatter_dimension=1, tiled=True)  143 us
    reduce_scatter x1, waiting for transfers between devices, body(): lax.psum_scatter(proj_grad, 'dp', scatter_dimension=1, tiled=True)  128 us
    psum x1, blocking collectives, body(): lax.psum((first_gain_grad, first_shift_grad, qkv_bias_grad, rope_freqs_gr...  79.5 us
    unnamed x10, waiting for transfers between devices  72.7 us
    psum x2, waiting for transfers between devices, run_forward(): lax.psum(jnp.dot(attended_low, weight_proj, preferred_element_type=jnp.fl...  50.6 us
    sub x2, other arithmetic, one_block(): exp_scores = jnp.exp(scores - row_max)  33.5 us
    dynamic_update_slice x4, local copies, waits for them, and re-layouts, attend_forward(): block_outs, log_sum = lax.map(one_block, (query_blocks, segment_blocks))  33.3 us
  transfers between devices with their start and end apart: 9, of which 8 were waited for; matrix products, arithmetic and copies ran while one was open for 5% of the time, Pallas kernels for 0%

commit v1 on v0

--- a/solution.py
+++ b/solution.py
@@ -6,6 +6,11 @@
 
 eps = 1e-06
 masked_score = -1e30
+
+
+def try_all_the_leaf(x_in, across):
+    finding = jax.lax.all_gather(x_in, axis_name=across)
+    return jnp.sum(finding, 0)
 
 
 def positions(image_grids, row_count):
@@ -199,7 +204,9 @@
     attended, log_sum = attend_forward(query_low, key_low, value_low, segment, cosine.shape[1])
     attended_low = attended.astype(jnp.bfloat16)
     branch = (
-        lax.psum(jnp.dot(attended_low, weight_proj, preferred_element_type=jnp.float32), "head")
+        try_all_the_leaf(
+            jnp.dot(attended_low, weight_proj, preferred_element_type=jnp.float32), "head"
+        )
         + bias_proj
     )
     middle = start_value + branch

time: 1090 us -> 1080 us (level)
  waiting for transfers between devices: 587 us -> 574 us
    psum x2 -> x0, waiting for transfers between devices: 50.6 us -> none  [run_forward(): lax.psum(jnp.dot(attended_low, weight_proj, preferred_element_type=jnp.fl...]
    all_gather x0 -> x2, waiting for transfers between devices: none -> 37.3 us  [try_all_the_leaf(): finding = jax.lax.all_gather(x_in, axis_name=across)]
where the time goes in v1:
time: 1080 us
  waiting for transfers between devices  574 us (53%)
  matrix products  180 us (17%)
  other arithmetic  131 us (12%)
  local copies, waits for them, and re-layouts  93.8 us (9%)
  blocking collectives  79.4 us (7%)
  between operations  15.7 us (1%)
    reduce_scatter x1, waiting for transfers between devices, body(): lax.psum_scatter(expand_grad, 'dp', scatter_dimension=0, tiled=True)  144 us
    reduce_scatter x1, waiting for transfers between devices, body(): lax.psum_scatter(contract_grad, 'dp', scatter_dimension=1, tiled=True)  143 us
    reduce_scatter x1, waiting for transfers between devices, body(): lax.psum_scatter(proj_grad, 'dp', scatter_dimension=1, tiled=True)  128 us
    psum x1, blocking collectives, body(): lax.psum((first_gain_grad, first_shift_grad, qkv_bias_grad, rope_freqs_gr...  79.4 us
    unnamed x10, waiting for transfers between devices  72.8 us
    all_gather x2, waiting for transfers between devices, try_all_the_leaf(): finding = jax.lax.all_gather(x_in, axis_name=across)  37.3 us
    dynamic_update_slice x4, local copies, waits for them, and re-layouts, attend_forward(): block_outs, log_sum = lax.map(one_block, (query_blocks, segment_blocks))  33.4 us
    sub x2, other arithmetic, one_block(): exp_scores = jnp.exp(scores - row_max)  33.3 us
  transfers between devices with their start and end apart: 9, of which 8 were waited for; matrix products, arithmetic and copies ran while one was open for 5% of the time, Pallas kernels for 0%

profile of v1, /device:TPU:0, one launch (start us, length us, event | category | flops | bytes accessed | tf_op | source)
XLA Modules:
  0.0 1075.8 jit_solution(6451969139869441404)
XLA Ops:
  13.6 3.8 add_bitcast_fusion.1
  19.4 4.8 subtract_convert_fusion.1
  29.9 64.1 %while.37 = (s32[]{:T(128)}, bf16[2,512,6,64]{1,3,2,0:T(8,128)(2,1)}, s32[2,512]{1,0:T(2,128)S(1)}, s32[1024]{0:T(1024)S(1)}, bf16[2,512,6,64]{1,3,2,0:T(8,128)(...) while((s32[]{:T(128)}, bf16[2,512,6,64]{1,3,2,0:T(8,128)(2,1)}, ...), condition=%wide.region_9.10_spmd, body=%wide.region_6.9_spmd.sunk | while | flops 830997504 | bytes 63609020 | solution.py:115
  30.2 7.4 fusion.243
  37.6 16.7 %fusion.244 = (f32[6,512]{1,0:T(8,128)S(1)}, f32[6,512,1024]{2,1,0:T(8,128)}) fusion(f32[6,512,1024]{2,1,0:T(8,128)} %fusion.243, pred[512,1024]{1,0:T(8,128)(4,1)S(1)} %broadcast_compare_fusion.8), kind=kOutput, calls=%fused_computation.303.clone.1 | output fusion | flops 18875392 | bytes 25702400 | tf_op jit(solution)/shard_map/while/body/eval_jaxpr/sub | solution.py:107
  54.3 6.7 fusion.245
  62.3 7.4 fusion.243
  69.7 16.7 %fusion.244 = (f32[6,512]{1,0:T(8,128)S(1)}, f32[6,512,1024]{2,1,0:T(8,128)}) fusion(f32[6,512,1024]{2,1,0:T(8,128)} %fusion.243, pred[512,1024]{1,0:T(8,128)(4,1)S(1)} %broadcast_compare_fusion.8), kind=kOutput, calls=%fused_computation.303.clone.1 | output fusion | flops 18875392 | bytes 25702400 | tf_op jit(solution)/shard_map/while/body/eval_jaxpr/sub | solution.py:107
  86.3 6.7 fusion.245
  99.0 19.4 %all-gather.5.cloned.1.call-done = f32[2048,768]{1,0:T(8,128)} async-done(((f32[1024,768]{1,0:T(8,128)}), f32[2048,768]{1,0:T(8,128)}) %all-gather.5.cloned.1.call-update) | async-done | bytes 6291472 | tf_op jit(solution)/shard_map/all_gather | solution.py:12
  118.4 5.2 reduce_sum.257
  128.3 21.5 %fusion.87 = f32[1024,768]{1,0:T(8,128)} fusion(bf16[1536,768]{1,0:T(8,128)(2,1)} %param.36, bf16[768,1536]{1,0:T(8,128)(2,1)S(1)} %copy-done, f32[1536]{0:T(1024)S(1)} %copy-done.71, f32[768]{0:T(1024)S(1)} %copy-done.79, f32[768]{0:T(1024)S(1)} %copy-done.56, f32[1024]{0:T(1024)S(1)} %add_rsqrt_fusion.2, f32[1024]{0:T(1024)S(1)} %broadcast_multiply_fusion.6, ...), kind=kOutput, calls=%fused_computation.148 | convolution fusion | flops 4941938688 | bytes 12606464 | tf_op jit(solution)/shard_map/dot_general | solution.py:218
  150.3 24.2 %all-reduce.7.cloned.1.call-done = f32[1024,768]{1,0:T(8,128)} async-done(((f32[1024,768]{1,0:T(8,128)}), f32[1024,768]{1,0:T(8,128)}) %all-reduce.7.cloned.1.call-update) | async-done | bytes 3145744 | tf_op jit(solution)/shard_map/psum | solution.py:218
  174.5 5.1 add_convert_fusion.2
  196.9 25.5 %while.38 = (s32[]{:T(128)}, bf16[2,512,6,64]{1,3,2,0:T(8,128)(2,1)}, f32[2,6,512]{2,1,0:T(8,128)S(1)}, s32[2,512]{1,0:T(2,128)S(1)}, s32[1024]{0:T(1024)S(1)}, ...) while((s32[]{:T(128)}, ...), condition=%wide.region_19.20_spmd, body=%wide.region_16.19_spmd.sunk | while | flops 843576320 | bytes 52164808 | solution.py:115
  204.3 4.4 fusion.250
  217.1 4.4 fusion.250
  228.4 17.9 %all-gather.7.cloned.1.call-done = f32[2048,768]{1,0:T(8,128)} async-done(((f32[1024,768]{1,0:T(8,128)}), f32[2048,768]{1,0:T(8,128)}) %all-gather.7.cloned.1.call-update) | async-done | bytes 6291472 | tf_op jit(solution)/shard_map/all_gather | solution.py:12
  246.2 5.2 reduce_sum.262
  255.1 15.1 %fusion.51 = (f32[1024,1536]{1,0:T(8,128)S(1)}, f32[1024,1536]{1,0:T(8,128)S(1)}) fusion(f32[1536]{0:T(1024)S(1)} %copy-done.72, bf16[768,1536]{1,0:T(8,128)(2,1)S(1)} %copy-done, f32[1024,768]{1,0:T(8,128)S(1)} %get-tuple-element.484, f32[768]{0:T(1024)S(1)} %copy-done.80, f32[768]{0:T(1024)S(1)} %copy-done.57, f32[1024]{0:T(1024)S(1)} %add_rsqrt_fusion, ...), kind=kOutput, calls=%fused_computation.70 | convolution fusion | flops 2518941696 | bytes 18108416 | tf_op jit(solution)/shard_map/dot_general | solution.py:215
  270.3 5.6 convert_reduce_fusion
  277.6 4.3 fusion.186
  282.0 24.6 %all-reduce.9.cloned.1.call-done = f32[1024,768]{1,0:T(8,128)} async-done(((f32[1024,768]{1,0:T(8,128)}), f32[1024,768]{1,0:T(8,128)}) %all-reduce.9.cloned.1.call-update) | async-done | bytes 3145744 | tf_op jit(solution)/shard_map/psum | solution.py:318
  306.6 4.5 multiply_reduce_fusion.1
  311.3 3.9 convert_reduce_fusion.5
  326.5 88.0 %while.39 = (s32[]{:T(128)}, f32[1024,6,64]{0,2,1:T(8,128)}, f32[1024,6,64]{0,2,1:T(8,128)}, f32[2,512,6,64]{1,0,3,2:T(2,128)}, bf16[2,512,6,64]{1,3,2,0:T(8,128...) while((s32[]{:T(128)}, f32[1024,6,64]{0,2,1:T(8,128)}, ...), condition=%wide.region_28.29_spmd.clone, body=%wide.region_26.28_spmd.clone.sunk | while | flops 2063135744 | bytes 132749616 | solution.py:166
  330.2 4.6 bitcast_add_fusion.5
  334.8 7.2 multiply_reduce_fusion.8
  342.0 6.9 multiply_convert_fusion.4
  355.1 15.0 %dynamic_update_slice.25 = f32[2,512,6,64]{1,0,3,2:T(2,128)} dynamic-update-slice(f32[2,512,6,64]{1,0,3,2:T(2,128)} %get-tuple-element.762, f32[1,512,6,64]{1,0,3,2:T(1,128)} %copy.269, s32[]{:T(128)S(6)} %copy.295, s32[]{:T(128)} %constant.51.clone.1..sunk, s32[]{:T(128)} %constant.51.clone.1..sunk, s32[]{:T(128)} %constant.51.clone.1..sunk) | dynamic-update-slice | bytes 1572868 | tf_op jit(solution)/shard_map/while/body/jit(dynamic_update_index_in_dim)/dynamic_update_slice | solution.py:115
  373.4 5.8 bitcast_add_fusion.5
  379.2 7.2 multiply_reduce_fusion.8
  386.4 6.9 multiply_convert_fusion.4
  399.5 15.0 %dynamic_update_slice.25 = f32[2,512,6,64]{1,0,3,2:T(2,128)} dynamic-update-slice(f32[2,512,6,64]{1,0,3,2:T(2,128)} %get-tuple-element.762, f32[1,512,6,64]{1,0,3,2:T(1,128)} %copy.269, s32[]{:T(128)S(6)} %copy.295, s32[]{:T(128)} %constant.51.clone.1..sunk, s32[]{:T(128)} %constant.51.clone.1..sunk, s32[]{:T(128)} %constant.51.clone.1..sunk) | dynamic-update-slice | bytes 1572868 | tf_op jit(solution)/shard_map/while/body/jit(dynamic_update_index_in_dim)/dynamic_update_slice | solution.py:115
  418.1 5.4 fusion.119
  435.4 5.9 convolution_bitcast_fusion.1
  442.0 6.1 convolution_bitcast_fusion
  448.1 6.5 copy.223
  455.8 3.9 fusion.142
  460.0 11.4 %fusion.84 = f32[1536,768]{0,1:T(8,128)} fusion(f32[1024,1536]{1,0:T(8,128)} %copy-done.83, f32[1024,1536]{1,0:T(8,128)} %copy-done.84, f32[1536]{0:T(1024)S(1)} %copy-done.73, bf16[1024,768]{1,0:T(8,128)(2,1)} %param.24, bf16[1024]{0:T(1024)(128)(2,1)S(1)} %copy-done.65), kind=kOutput, calls=%fused_computation.133 | convolution fusion | flops 2422996992 | bytes 18882560 | tf_op jit(solution)/shard_map/tf,td->fd/dot_general | solution.py:308
  472.1 8.0 fusion.177
  482.0 5.8 fusion.111
  494.9 79.4 %all-reduce.1 = (f32[768]{0:T(1024)}, f32[768]{0:T(1024)}, f32[3,384]{1,0:T(4,128)}, f32[2,6,32]{2,1,0:T(8,128)S(1)}, f32[768]{0:T(1024)}, /*index=5*/f32[768]{0...) all-reduce(f32[768]{0:T(1024)S(1)} %get-tuple-element.410, ...), channel_id=1, replica_groups=mesh['dp'=16,'head'=2] {'dp'}, use_global_device_ids=true, to_apply=%region_37.38 | all-reduce | flops 7680 | bytes 61440 | tf_op jit(solution)/shard_map/psum | solution.py:373
  574.9 5.0 fusion.77
  579.9 72.7 %all-reduce.13.cloned.1.call-done = f32[3,768,384]{2,0,1:T(4,128)} async-done(((f32[3,768,384]{2,0,1:T(4,128)}), f32[3,768,384]{2,0,1:T(4,128)}) %all-reduce.13.cloned.1.call-update) | async-done | bytes 3538960
  654.3 127.7 %reduce-scatter.4.cloned.1.call-done = f32[384,48]{0,1:T(8,128)} async-done(((f32[384,768]{0,1:T(8,128)}), f32[384,48]{0,1:T(8,128)}) %reduce-scatter.4.cloned.1.call-update) | async-done | bytes 73744 | tf_op jit(solution)/shard_map/reduce_scatter | solution.py:359
  782.0 143.5 %reduce-scatter.8.cloned.1.call-done = f32[1536,48]{0,1:T(8,128)} async-done(((f32[1536,768]{0,1:T(8,128)}), f32[1536,48]{0,1:T(8,128)}) %reduce-scatter.8.cloned.1.call-update) | async-done | bytes 294928 | tf_op jit(solution)/shard_map/reduce_scatter | solution.py:361
  925.5 143.6 %reduce-scatter.6.cloned.1.call-done = f32[48,1536]{1,0:T(8,128)} async-done(((f32[768,1536]{1,0:T(8,128)}), f32[48,1536]{1,0:T(8,128)}) %reduce-scatter.6.cloned.1.call-update) | async-done | bytes 294928 | tf_op jit(solution)/shard_map/reduce_scatter | solution.py:360
  (323 shorter events, 130.8 us)
Async XLA Ops:
  7.2 121.1 %copy-start = (bf16[768,1536]{1,0:T(8,128)(2,1)S(1)}, bf16[768,1536]{1,0:T(8,128)(2,1)}, u32[]{:S(2)}) copy-start(bf16[768,1536]{1,0:T(8,128)(2,1)} %param.34) | copy-start | bytes 7077892
  7.2 6.4 copy-start.59
  7.2 6.4 copy-start.74
  7.2 6.4 copy-start.76
  7.2 111.2 %all-gather.5.cloned.1.call-start = ((), (), s32[]{:S(2)}) async-start(), calls=%async_computation.9 | async-start | bytes 9437184 | tf_op jit(solution)/shard_map/all_gather | solution.py:12
  9.7 3.9 copy-start.1
  19.1 5.1 copy-start.39
  19.1 5.0 copy-start.42
  19.4 4.8 copy-start.33
  19.4 4.8 copy-start.36
  37.6 16.7 %copy-start.25 = (bf16[2,512,6,64]{1,3,2,0:T(8,128)(2,1)S(1)}, bf16[2,512,6,64]{1,3,2,0:T(8,128)(2,1)}, u32[]{:S(2)}) copy-start(bf16[2,512,6,64]{1,3,2,0:T(8,128)(2,1)} %get-tuple-element.704) | copy-start | bytes 2359300 | tf_op jit(solution)/shard_map/while
  37.6 16.7 %copy-start.32 = (bf16[1024,6,64]{0,2,1:T(8,128)(2,1)S(1)}, bf16[1024,6,64]{0,2,1:T(8,128)(2,1)}, u32[]{:S(2)}) copy-start(bf16[1024,6,64]{0,2,1:T(8,128)(2,1)} %get-tuple-element.717) | copy-start | bytes 2359300 | tf_op jit(solution)/shard_map/while
  69.7 16.7 %copy-start.25 = (bf16[2,512,6,64]{1,3,2,0:T(8,128)(2,1)S(1)}, bf16[2,512,6,64]{1,3,2,0:T(8,128)(2,1)}, u32[]{:S(2)}) copy-start(bf16[2,512,6,64]{1,3,2,0:T(8,128)(2,1)} %get-tuple-element.704) | copy-start | bytes 2359300 | tf_op jit(solution)/shard_map/while
  69.7 16.7 %copy-start.32 = (bf16[1024,6,64]{0,2,1:T(8,128)(2,1)S(1)}, bf16[1024,6,64]{0,2,1:T(8,128)(2,1)}, u32[]{:S(2)}) copy-start(bf16[1024,6,64]{0,2,1:T(8,128)(2,1)} %get-tuple-element.717) | copy-start | bytes 2359300 | tf_op jit(solution)/shard_map/while
  98.8 75.6 %all-reduce.7.cloned.1.call-start = ((), (), s32[]{:S(2)}) async-start(), calls=%async_computation.3 | async-start | bytes 6291456 | tf_op jit(solution)/shard_map/psum | solution.py:218
  118.4 5.2 copy-start.49
  149.8 24.7 %copy-start.68 = (f32[768]{0:T(1024)S(1)}, f32[768]{0:T(1024)}, u32[]{:S(2)}) copy-start(f32[768]{0:T(1024)} %param.37) | copy-start | bytes 9220
  149.8 96.4 %all-gather.7.cloned.1.call-start = ((), (), s32[]{:S(2)}) async-start(), calls=%async_computation.10 | async-start | bytes 9437184 | tf_op jit(solution)/shard_map/all_gather | solution.py:12
  174.5 5.1 copy-start.3
  179.9 4.0 copy-start.45
  185.3 4.0 copy-start.14
  185.3 4.0 copy-start.15
  228.1 78.5 %all-reduce.9.cloned.1.call-start = ((), (), s32[]{:S(2)}) async-start(), calls=%async_computation.4 | async-start | bytes 6291456 | tf_op jit(solution)/shard_map/psum | solution.py:318
  254.3 15.9 %copy-start.9 = (f32[1024,768]{1,0:T(8,128)}, f32[1024,768]{1,0:T(8,128)S(1)}, u32[]{:S(2)}) copy-start(f32[1024,768]{1,0:T(8,128)S(1)} %get-tuple-element.484) | copy-start | bytes 9437188
  254.3 56.7 %copy-start.47 = (f32[1024]{0:T(1024)}, f32[1024]{0:T(1024)S(1)}, u32[]{:S(2)}) copy-start(f32[1024]{0:T(1024)S(1)} %broadcast_multiply_fusion.4) | copy-start | bytes 12292
  255.1 55.9 %copy-start.52 = (f32[1024]{0:T(1024)}, f32[1024]{0:T(1024)S(1)}, u32[]{:S(2)}) copy-start(f32[1024]{0:T(1024)S(1)} %add_rsqrt_fusion) | copy-start | bytes 12292
  255.1 15.1 %copy-start.31 = (bf16[1024,768]{1,0:T(8,128)(2,1)S(1)}, bf16[1024,768]{1,0:T(8,128)(2,1)}, u32[]{:S(2)}) copy-start(bf16[1024,768]{1,0:T(8,128)(2,1)} %param.24) | copy-start | bytes 4718596
  255.1 15.1 %copy-start.64 = (bf16[1024]{0:T(1024)(128)(2,1)S(1)}, bf16[1024]{0:T(1024)(128)(2,1)}, u32[]{:S(2)}) copy-start(bf16[1024]{0:T(1024)(128)(2,1)} %get-tuple-element.481) | copy-start | bytes 6148
  255.1 15.2 %copy-start.69 = (bf16[1536,768]{1,0:T(8,128)(2,1)S(1)}, bf16[1536,768]{1,0:T(8,128)(2,1)}, u32[]{:S(2)}) copy-start(bf16[1536,768]{1,0:T(8,128)(2,1)} %param.36) | copy-start | bytes 7077892
  270.2 5.7 copy-start.83
  270.2 5.7 copy-start.84
  282.0 209.6 %all-reduce.11.cloned.1.call-start = ((), (), s32[]{:S(2)}) async-start(), calls=%async_computation.5 | async-start | bytes 6291456 | tf_op jit(solution)/shard_map/psum | solution.py:350
  306.6 4.5 copy-start.10
  306.6 4.7 copy-start.16
  311.3 5.5 copy-start.22
  330.2 4.6 copy-start.13
  373.4 5.8 copy-start.13
  418.1 5.4 copy-start.6
  430.5 4.9 copy-start.27
  441.3 211.3 %all-reduce.13.cloned.1.call-start = ((), (), s32[]{:S(2)}) async-start(), calls=%async_computation.11 | async-start | bytes 9437184
  454.6 5.3 copy-start.65
  454.7 5.3 copy-start.73
  454.7 327.3 %reduce-scatter.4.cloned.1.call-start = ((), (), s32[]{:S(2)}) async-start(), calls=%async_computation.6 | async-start | bytes 1253376 | tf_op jit(solution)/shard_map/reduce_scatter | solution.py:359
  459.7 465.8 %reduce-scatter.8.cloned.1.call-start = ((), (), s32[]{:S(2)}) async-start(), calls=%async_computation.8 | async-start | bytes 5013504 | tf_op jit(solution)/shard_map/reduce_scatter | solution.py:361
  471.4 597.6 %reduce-scatter.6.cloned.1.call-start = ((), (), s32[]{:S(2)}) async-start(), calls=%async_computation.7 | async-start | bytes 5013504 | tf_op jit(solution)/shard_map/reduce_scatter | solution.py:360
  482.0 9.2 copy-start.28
  482.0 9.2 copy-start.29
  482.0 9.2 copy-start.30
  (58 other events, 109.7 us)
Sparse Core Ops, SparseCore 0:
  98.9 19.4 all-gather.4
  149.9 24.4 all-reduce.6
  228.2 17.9 all-gather.6
  282.1 24.4 all-reduce.8
  441.4 24.4 all-reduce.10
  471.5 181.0 all-reduce.12
  657.9 124.0 reduce-scatter.3
  787.7 137.6 reduce-scatter.7
  931.2 137.7 reduce-scatter.5
